TPU v7x, 32 devices: a whole 2x2x4 slice. The times are simulated.
32 devices in a mesh: groups: 2 (over y), ctx: 4 (over z), head: 2 (over x), rep: 2 (over core).
Axes of the slice: x: 2, y: 2, z: 4, core: 2. Of those that a mesh axis runs over, the one named last changes fastest.
Arguments:
- queries: bfloat16 [8192, 16, 2, 128], P(('groups', 'ctx'), 'head', 'rep'), parts along dimension 0, may hold values from -10 to 10
- keys_values: bfloat16 [2, 8192, 16, 128], P('rep', ('groups', 'ctx'), 'head'), parts along dimension 1, may hold values from -6 to 6
- far_list: int32 [64, 16], P('groups'), parts along dimension 0, may hold values from 0 to 31, as said below
- far_count: int32 [64], P('groups'), parts along dimension 0, may hold values from 0 to 8
Outputs:
- attended: bfloat16 [8192, 16, 2, 128], P(('groups', 'ctx'), 'head', 'rep'), parts along dimension 0
There are 2 independent parts, one for each index of `groups`. A program takes and returns all parts, laid end to end along the dimension named above; each array names one. Nothing has to cross between parts.
Inputs may be any that keep to these rules, and one draw needn't show every extreme that they name: `far_list`: for query block c, the entries j < far_count[c] are distinct block numbers no later than c - 4; entries from far_count[c] on are arbitrary and not read. Taken over all query blocks of one span of 1024 tokens, the counted entries name at most 2 distinct blocks of any one span, and some span's query blocks name exactly 2 of some span in every draw.
All inputs are finite; a program needn't handle non-finite values.
Results may differ from a plain program's by a relative error of at most 0.003.
Values may be sent and summed in bfloat16 or wider, within the bound.
A program may use at most 128 MiB of HBM per device.

v0:
```python
import jax
import jax.numpy as jnp
from jax import lax
from jax.sharding import PartitionSpec as P

BLK = 128
WB = 4
FSEL = 16
CAP = 2
floor_score = -1e30
score_scale = 1.0 / 12.0


def partner(block, axis, stride):
    count = lax.axis_size(axis)
    route = []
    for low in range(count):
        high = low | 1 << stride
        if high != low and high < count:
            route += [(low, high), (high, low)]
    return lax.ppermute(block, axis, route)


def from_behind(x, axis, by):
    count = lax.axis_size(axis)
    pairs = [(i, i + by) for i in range(count) if 0 <= i + by < count]
    return lax.ppermute(x, axis, pairs)


def group_weights(scores, usable):
    masked = jnp.where(usable, scores, floor_score)
    summit = jnp.max(masked, axis=-1, keepdims=True)
    weights = jnp.where(usable, jnp.exp(masked - summit), 0.0)
    return (summit, weights, jnp.sum(weights, axis=-1, keepdims=True))


def row_major(stacked):
    return jnp.moveaxis(stacked, 0, 2).reshape(
        stacked.shape[1], stacked.shape[2], stacked.shape[0] * stacked.shape[3], stacked.shape[-1]
    )


def local(queries, keys_values, far_list, far_count):
    tok_rows, head_count, query_group, head_width = queries.shape
    block_len = BLK
    own_blocks = tok_rows // block_len
    span_count = lax.axis_size("ctx")
    my_span = lax.axis_index("ctx")
    my_side = lax.axis_index("rep")
    rim_len = (WB - 1) * block_len
    rim_start = tok_rows - rim_len
    other_half = partner(keys_values, "rep", 0)
    local_pair = jnp.concatenate(
        [
            jnp.where(my_side == 0, keys_values, other_half),
            jnp.where(my_side == 0, other_half, keys_values),
        ],
        axis=0,
    )
    slot_range = jnp.arange(FSEL, dtype=jnp.int32)
    block_index = jnp.arange(own_blocks, dtype=jnp.int32)
    my_blocks = my_span * own_blocks + block_index
    counted = slot_range[None, :] < far_count[:, None]
    every_block = jnp.arange(span_count * own_blocks, dtype=jnp.int32)
    list_blocks = far_list.reshape(span_count, own_blocks, FSEL)
    counted_blocks = counted.reshape(span_count, own_blocks, FSEL)
    flat_lists = list_blocks.reshape(span_count, -1)
    flat_counted = counted_blocks.reshape(span_count, -1)
    wanted = jnp.any(
        (flat_lists[:, :, None] == my_blocks[None, None, :]) & flat_counted[:, :, None], axis=1
    )
    wanted_rank = jnp.cumsum(wanted.astype(jnp.int32), axis=1) - 1
    in_slot = wanted[:, None, :] & (
        wanted_rank[:, None, :] == jnp.arange(CAP, dtype=jnp.int32)[None, :, None]
    )
    send_index = jnp.sum(jnp.where(in_slot, block_index[None, None, :], 0), axis=2).reshape(-1)
    slot_width = CAP
    rim_pair = from_behind(local_pair[:, rim_start:], "ctx", 1)
    blocked = local_pair.reshape(local_pair.shape[0], own_blocks, block_len, head_count, head_width)
    pool_pair = lax.all_to_all(
        jnp.take(blocked, send_index, axis=1), "ctx", split_axis=1, concat_axis=1, tiled=True
    )
    my_list = lax.dynamic_slice_in_dim(far_list, my_span * own_blocks, own_blocks, 0)
    my_count = lax.dynamic_slice_in_dim(far_count, my_span * own_blocks, own_blocks, 0)
    my_counted = slot_range[None, :] < my_count[:, None]
    extended = jnp.concatenate([rim_pair, local_pair], axis=1)
    query_rows = min(4 * block_len, tok_rows)
    key_rows = query_rows + rim_len
    base_pos = my_span * tok_rows

    def near_part(first_row):
        query_tile = lax.dynamic_slice_in_dim(queries, first_row, query_rows, 0)
        pair_tile = lax.dynamic_slice_in_dim(extended, first_row, key_rows, 1)
        scores = (
            jnp.einsum(
                "qhgd,khd->hgqk", query_tile, pair_tile[0], preferred_element_type=jnp.float32
            )
            * score_scale
        )
        query_pos = first_row + jnp.arange(query_rows, dtype=jnp.int32)
        key_pos = first_row - rim_len + jnp.arange(key_rows, dtype=jnp.int32)
        usable = (
            (key_pos[None, :] <= query_pos[:, None])
            & (key_pos[None, :] // block_len >= query_pos[:, None] // block_len - WB + 1)
            & (base_pos + key_pos[None, :] >= 0)
        )
        summit, weights, weight_sum = group_weights(scores, usable)
        mixed_out = jnp.einsum(
            "hgqk,khd->hgqd",
            weights.astype(jnp.bfloat16),
            pair_tile[1],
            preferred_element_type=jnp.float32,
        )
        return (summit, mixed_out, weight_sum)

    starts = jnp.arange(tok_rows // query_rows, dtype=jnp.int32) * query_rows
    near_top, near_out, near_sum = lax.map(near_part, starts)
    far_keys_len = FSEL * block_len
    query_blocks = queries.reshape(own_blocks, block_len, head_count, query_group, head_width)
    named_block = (my_list.reshape(-1)[:, None] == every_block[None, :]) & my_counted.reshape(-1)[
        :, None
    ]
    needed = jnp.any(named_block, axis=0).reshape(span_count, own_blocks)
    place = (
        jnp.cumsum(needed.astype(jnp.int32), axis=1)
        - 1
        + 0
        + jnp.arange(span_count, dtype=jnp.int32)[:, None] * slot_width
    )
    own_slots = jnp.sum(jnp.where(named_block, place.reshape(-1)[None, :], 0), axis=1).reshape(
        my_list.shape[0], FSEL
    )
    total = query_blocks.shape[0]
    width_step = 4
    turns = total // width_step

    def far_group(task):
        query_tile, slot_tile, live = task
        keys_tile = jnp.take(pool_pair[0], slot_tile.reshape(-1), axis=0).reshape(
            width_step, far_keys_len, head_count, head_width
        )
        value_tile = jnp.take(pool_pair[1], slot_tile.reshape(-1), axis=0).reshape(
            width_step, far_keys_len, head_count, head_width
        )
        scores = (
            jnp.einsum(
                "bqhgd,bkhd->bhgqk", query_tile, keys_tile, preferred_element_type=jnp.float32
            )
            * score_scale
        )
        usable = jnp.repeat(slot_range[None, :] < live[:, None], block_len, axis=1)[
            :, None, None, None, :
        ]
        summit, weights, weight_sum = group_weights(scores, usable)
        mixed_out = jnp.einsum(
            "bhgqk,bkhd->bhgqd",
            weights.astype(jnp.bfloat16),
            value_tile,
            preferred_element_type=jnp.float32,
        )
        return (summit, mixed_out, weight_sum)

    grouped = (
        query_blocks.reshape((turns, width_step) + query_blocks.shape[1:]),
        own_slots.reshape(turns, width_step, FSEL),
        my_count.reshape(turns, width_step),
    )
    results = lax.map(far_group, grouped)
    own_top, own_out, own_sum = tuple(
        (piece.reshape((total,) + piece.shape[2:]) for piece in results)
    )
    far_top, far_out, far_sum = (row_major(own_top), row_major(own_out), row_major(own_sum))
    near_top, near_out, near_sum = (row_major(near_top), row_major(near_out), row_major(near_sum))
    summit = jnp.maximum(near_top, far_top)
    near_scale = jnp.exp(near_top - summit)
    far_scale = jnp.exp(far_top - summit)
    result = (near_scale * near_out + far_scale * far_out) / (
        near_scale * near_sum + far_scale * far_sum
    )
    return jnp.transpose(result, (2, 0, 1, 3)).astype(jnp.bfloat16)


def solution(mesh):
    in_specs = (
        P(("groups", "ctx"), "head", "rep", None),
        P("rep", ("groups", "ctx"), "head", None),
        P("groups", None),
        P("groups"),
    )
    out_specs = P(("groups", "ctx"), "head", "rep", None)
    return jax.shard_map(local, mesh=mesh, in_specs=in_specs, out_specs=out_specs, check_vma=False)
```

profile of v0, /device:TPU:24, one launch (start us, length us, event | category | flops | bytes accessed | tf_op | source)
XLA Modules:
  0.0 359.6 jit_solution(871911679812161485)
XLA Ops:
  0.0 1.9 copy.46
  2.0 0.7 lt.111
  2.9 0.8 copy.50
  4.6 0.7 dynamic_slice.49
  5.6 0.8 constant_dynamic-slice_fusion.4
  7.0 2.9 broadcast_select_fusion.3
  9.8 1.3 copy-done.1
  11.2 1.3 fusion.48
  12.5 1.3 collective-permute-start.1
  14.8 2.0 pad_maximum_fusion
  16.7 4.6 %copy.52 = bf16[2,1024,8,128]{3,2,1,0:T(8,128)(2,1)} copy(bf16[2,1024,8,128]{3,1,2,0:T(8,128)(2,1)S(1)} %pad_maximum_fusion) | data formatting | bytes 8388608 | tf_op jit(solution)/shard_map/concatenate | solution.py:53
  21.4 5.2 %gather_fusion.2 = bf16[8,2,128,8,128]{4,3,2,1,0:T(8,128)(2,1)} fusion(bf16[2,8,128,8,128]{4,3,2,1,0:T(8,128)(2,1)} %bitcast.197, s32[1024]{0:T(1024)S(1)} %pad_clamp_fusion.1), kind=kCustom, calls=%fused_computation.2 | custom fusion | bytes 8388640 | tf_op jit(solution)/shard_map/jit(_take)/gather | solution.py:81
  26.6 4.6 %select_bitcast_fusion = bf16[2,8,128,8,128]{4,3,2,0,1:T(8,128)(2,1)} fusion(bf16[8,2,128,8,128]{4,3,2,1,0:T(8,128)(2,1)} %gather_fusion.2, pred[8]{0:T(512)(128)(4,1)S(1)} %compare_and_fusion.1), kind=kLoop, calls=%fused_computation.88 | loop fusion | flops 2097152 | bytes 8388616 | tf_op jit(solution)/shard_map/jit(_take)/select_n | solution.py:81
  31.2 8.4 %all-to-all-start = ((bf16[2,8,128,8,128]{4,3,2,0,1:T(8,128)(2,1)}), bf16[2,8,128,8,128]{4,3,2,0,1:T(8,128)(2,1)}, u32[]{:S(2)}, u32[]{:S(2)}) async-start(bf16[2,8,128,8,128]{4,3,2,0,1:T(8,128)(2,1)} %select_bitcast_fusion), calls=%async_computation | async-start | bytes 8388608 | tf_op jit(solution)/shard_map/all_to_all | solution.py:80
  39.6 12.3 %collective-permute-done.1 = bf16[2,384,8,128]{3,1,2,0:T(8,128)(2,1)} collective-permute-done((bf16[2,384,8,128]{3,1,2,0:T(8,128)(2,1)}, bf16[2,384,8,128]{3,1,2,0:T(8,128)(2,1)}, u32[]{:S(2)}, u32[]{:S(2)}) %collective-permute-start.1) | collective-permute-done | bytes 1572896 | tf_op jit(solution)/shard_map/ppermute | solution.py:27
  52.0 4.9 %maximum_maximum_fusion = bf16[2,1408,8,128]{3,1,2,0:T(8,128)(2,1)} fusion(bf16[1,1024,8,128]{3,1,2,0:T(8,128)(2,1)} %copy-done.1, bf16[1,1024,8,128]{3,1,2,0:T(8,128)(2,1)S(1)} %get-tuple-element.367, bf16[2,384,8,128]{3,1,2,0:T(8,128)(2,1)} %collective-permute-done.1), kind=kLoop, calls=%fused_computation.84 | loop fusion | flops 17301504 | bytes 11534336 | tf_op jit(solution)/shard_map/concatenate | solution.py:86
  56.9 72.9 %while.34 = (s32[]{:T(128)}, f32[2,8,1,512,1]{3,1,4,2,0:T(8,128)S(1)}, f32[2,8,1,512,128]{4,3,1,2,0:T(8,128)}, f32[2,8,1,512,1]{3,4,2,1,0:T(1,128)S(1)}, s32[2]{...) while((s32[]{:T(128)}, ...), condition=%wide.region_3.4_spmd, body=%wide.region_0.3_spmd.sunk | while | flops 1928610944 | bytes 54944268 | solution.py:117
  58.1 0.7 fusion.66
  58.8 0.9 and_and_fusion.2
  61.6 1.3 constant_dynamic-slice_fusion.8
  64.2 8.4 %fusion.67 = (f32[8,512]{1,0:T(8,128)S(1)}, f32[8,896,512]{2,1,0:T(8,128)}) fusion(pred[512,896]{0,1:T(8,128)(4,1)S(1)} %and_and_fusion.2, bf16[512,8,1,128]{3,1,2,0:T(8,128)(2,1)S(1)} %constant_dynamic-slice_fusion.8, bf16[2,1408,8,128]{3,1,2,0:T(8,128)(2,1)} %get-tuple-element.552, s32[]{:T(128)S(6)} %select_n.250), kind=kOutput, calls=%fused_computation.6.clone.1 | convolution fusion | flops 950530048 | bytes 18038788 | tf_op jit(solution)/shard_map/while/body/eval_jaxpr/qhgd,khd->hgqk/dot_general | solution.py:95
  72.6 8.7 %fusion.68 = f32[8,512]{1,0:T(8,128)S(1)} fusion(f32[8,896,512]{2,1,0:T(8,128)} %get-tuple-element.476, f32[8,512]{1,0:T(8,128)S(1)} %get-tuple-element.475, pred[512,896]{0,1:T(8,128)(4,1)S(1)} %and_and_fusion.2), kind=kLoop, calls=%fused_computation.7.clone.1 | loop fusion | flops 18345984 | bytes 15171584 | tf_op jit(solution)/shard_map/while/body/eval_jaxpr/reduce_sum | solution.py:34
  81.3 12.1 %bitcast_dynamic-update-slice_fusion.9 = f32[2,8,1,512,128]{4,3,1,2,0:T(8,128)} fusion(f32[2,8,1,512,128]{4,3,1,2,0:T(8,128)} %get-tuple-element.534, s32[]{:T(128)} %get-tuple-element.532, bf16[2,1408,8,128]{3,1,2,0:T(8,128)(2,1)} %get-tuple-element.552, s32[]{:T(128)S(6)} %add.369, s32[]{:T(128)S(6)} %select_n.250, ...), kind=kOutput, calls=%fused_computation.12.clone.1 | convolution fusion | flops 957874176 | bytes 19087880 | tf_op jit(solution)/shard_map/while/body/eval_jaxpr/hgqk,khd->hgqd/dot_general | solution.py:108
  95.3 0.9 and_and_fusion.2
  98.1 1.3 constant_dynamic-slice_fusion.8
  100.7 8.4 %fusion.67 = (f32[8,512]{1,0:T(8,128)S(1)}, f32[8,896,512]{2,1,0:T(8,128)}) fusion(pred[512,896]{0,1:T(8,128)(4,1)S(1)} %and_and_fusion.2, bf16[512,8,1,128]{3,1,2,0:T(8,128)(2,1)S(1)} %constant_dynamic-slice_fusion.8, bf16[2,1408,8,128]{3,1,2,0:T(8,128)(2,1)} %get-tuple-element.552, s32[]{:T(128)S(6)} %select_n.250), kind=kOutput, calls=%fused_computation.6.clone.1 | convolution fusion | flops 950530048 | bytes 18038788 | tf_op jit(solution)/shard_map/while/body/eval_jaxpr/qhgd,khd->hgqk/dot_general | solution.py:95
  109.1 8.7 %fusion.68 = f32[8,512]{1,0:T(8,128)S(1)} fusion(f32[8,896,512]{2,1,0:T(8,128)} %get-tuple-element.476, f32[8,512]{1,0:T(8,128)S(1)} %get-tuple-element.475, pred[512,896]{0,1:T(8,128)(4,1)S(1)} %and_and_fusion.2), kind=kLoop, calls=%fused_computation.7.clone.1 | loop fusion | flops 18345984 | bytes 15171584 | tf_op jit(solution)/shard_map/while/body/eval_jaxpr/reduce_sum | solution.py:34
  117.8 12.0 %bitcast_dynamic-update-slice_fusion.9 = f32[2,8,1,512,128]{4,3,1,2,0:T(8,128)} fusion(f32[2,8,1,512,128]{4,3,1,2,0:T(8,128)} %get-tuple-element.534, s32[]{:T(128)} %get-tuple-element.532, bf16[2,1408,8,128]{3,1,2,0:T(8,128)(2,1)} %get-tuple-element.552, s32[]{:T(128)S(6)} %add.369, s32[]{:T(128)S(6)} %select_n.250, ...), kind=kOutput, calls=%fused_computation.12.clone.1 | convolution fusion | flops 957874176 | bytes 19087880 | tf_op jit(solution)/shard_map/while/body/eval_jaxpr/hgqk,khd->hgqd/dot_general | solution.py:108
  130.4 6.5 %copy.59 = f32[8,1,2,512,128]{4,0,3,2,1:T(8,128)} copy(f32[8,1,2,512,128]{4,3,0,1,2:T(8,128)} %bitcast.198) | data formatting | bytes 8388608 | tf_op jit(solution)/shard_map/transpose | solution.py:38
  137.0 4.3 %all-to-all-done = bf16[2,8,128,8,128]{4,3,2,0,1:T(8,128)(2,1)} async-done(((bf16[2,8,128,8,128]{4,3,2,0,1:T(8,128)(2,1)}), bf16[2,8,128,8,128]{4,3,2,0,1:T(8,128)(2,1)}, u32[]{:S(2)}, u32[]{:S(2)}) %all-to-all-start) | async-done | bytes 4194336 | tf_op jit(solution)/shard_map/all_to_all | solution.py:80
  141.2 4.5 %copy.56 = bf16[2,8,128,8,128]{4,3,2,1,0:T(8,128)(2,1)} copy(bf16[2,8,128,8,128]{4,3,2,0,1:T(8,128)(2,1)} %all-to-all-done) | data formatting | bytes 8388608
  145.8 202.6 %while.35 = (s32[]{:T(128)}, f32[2,4,8,1,128,1]{4,2,1,5,3,0:T(8,128)S(1)}, f32[2,4,8,1,128,128]{5,4,2,1,3,0:T(8,128)}, f32[2,4,8,1,128,1]{4,5,3,2,1,0:T(1,128)S(...) while((s32[]{:T(128)}, ...), condition=%wide.region_13.15_spmd.clone, body=%wide.region_10.14_spmd.clone.sunk | while | flops 4420789760 | bytes 290651552 | solution.py:168
  145.9 3.9 %slice_bitcast_fusion.3 = (bf16[8,128,8,128]{3,2,1,0:T(8,128)(2,1)}, bf16[8,128,8,128]{3,2,1,0:T(8,128)(2,1)S(1)}) fusion(bf16[2,8,128,8,128]{4,3,2,1,0:T(8,128)(2,1)} %get-tuple-element.514), kind=kLoop, calls=%fused_computation.66.clone.1 | loop fusion | bytes 8388608 | tf_op jit(solution)/shard_map/while/body/eval_jaxpr/squeeze | solution.py:142
  149.8 8.9 %gather_fusion = bf16[64,128,8,128]{3,2,1,0:T(8,128)(2,1)} fusion(bf16[8,128,8,128]{3,2,1,0:T(8,128)(2,1)} %get-tuple-element.485, s32[1024]{0:T(1024)S(1)} %pad_clamp_fusion.3), kind=kCustom, calls=%fused_computation.1.clone.clone.1 | custom fusion | bytes 33554688 | tf_op jit(solution)/shard_map/while/body/eval_jaxpr/jit(_take)/gather | solution.py:142
  158.7 7.3 %gather_fusion.1 = bf16[64,128,8,128]{3,2,1,0:T(8,128)(2,1)} fusion(bf16[8,128,8,128]{3,2,1,0:T(8,128)(2,1)S(1)} %get-tuple-element.486, s32[1024]{0:T(1024)S(1)} %pad_clamp_fusion.3), kind=kCustom, calls=%fused_computation.clone.clone.1 | custom fusion | bytes 33554688 | tf_op jit(solution)/shard_map/while/body/eval_jaxpr/jit(_take)/gather | solution.py:139
  166.0 23.2 %broadcast_select_fusion.5 = (bf16[64,128,8,128]{3,2,1,0:T(8,128)(2,1)}, bf16[64,128,8,128]{3,2,1,0:T(8,128)(2,1)}) fusion(bf16[64,128,8,128]{3,2,1,0:T(8,128)(2,1)} %gather_fusion, pred[64]{0:T(512)(128)(4,1)S(1)} %compare_and_fusion.3, bf16[64,128,8,128]{3,2,1,0:T(8,128)(2,1)} %gather_fusion.1), kind=kLoop, calls=%fused_computation.61.clone.1 | loop fusion | flops 16777216 | bytes 67108928 | tf_op jit(solution)/shard_map/while/body/eval_jaxpr/jit(_take)/select_n | solution.py:142
  189.5 19.7 %bitcast_reduce_fusion.2 = (f32[4,8,128]{2,1,0:T(8,128)S(1)}, f32[4,8,2048,128]{3,2,1,0:T(8,128)}) fusion(pred[4,2048]{1,0:T(4,128)(4,1)S(1)} %bitcast.199, bf16[1,4,128,8,1,128]{5,3,2,1,0,4:T(8,128)(2,1)S(1)} %constant_dynamic-slice_fusion.9, bf16[4,2048,8,128]{3,2,1,0:T(8,128)(2,1)} %bitcast.193), kind=kOutput, calls=%fused_computation.47.clone.1 | convolution fusion | flops 2172645376 | bytes 51404800 | tf_op jit(solution)/shard_map/while/body/eval_jaxpr/bqhgd,bkhd->bhgqk/dot_general | solution.py:146
  209.2 15.1 %fusion.72 = f32[4,8,128]{2,1,0:T(8,128)S(1)} fusion(f32[4,8,2048,128]{3,2,1,0:T(8,128)} %get-tuple-element.490, f32[4,8,128]{2,1,0:T(8,128)S(1)} %get-tuple-element.488, pred[4,2048]{1,0:T(4,128)(4,1)S(1)} %bitcast.200), kind=kLoop, calls=%fused_computation.51.clone.1 | loop fusion | flops 41938944 | bytes 33595392 | tf_op jit(solution)/shard_map/while/body/eval_jaxpr/reduce_sum | solution.py:34
  224.3 22.7 %bitcast_dynamic-update-slice_fusion.11 = f32[2,4,8,1,128,128]{5,4,2,1,3,0:T(8,128)} fusion(f32[2,4,8,1,128,128]{5,4,2,1,3,0:T(8,128)} %get-tuple-element.502, s32[]{:T(128)} %get-tuple-element.500, bf16[4,2048,8,128]{3,2,1,0:T(8,128)(2,1)} %bitcast.192, f32[4,8,2048,128]{3,2,1,0:T(8,128)} %get-tuple-element.490, ...), kind=kOutput, calls=%fused_computation.65.clone.1 | convolution fusion | flops 2189426688 | bytes 52462080 | tf_op jit(solution)/shard_map/while/body/eval_jaxpr/bhgqk,bkhd->bhgqd/dot_general | solution.py:155
  247.1 3.9 %slice_bitcast_fusion.3 = (bf16[8,128,8,128]{3,2,1,0:T(8,128)(2,1)}, bf16[8,128,8,128]{3,2,1,0:T(8,128)(2,1)S(1)}) fusion(bf16[2,8,128,8,128]{4,3,2,1,0:T(8,128)(2,1)} %get-tuple-element.514), kind=kLoop, calls=%fused_computation.66.clone.1 | loop fusion | bytes 8388608 | tf_op jit(solution)/shard_map/while/body/eval_jaxpr/squeeze | solution.py:142
  251.1 8.9 %gather_fusion = bf16[64,128,8,128]{3,2,1,0:T(8,128)(2,1)} fusion(bf16[8,128,8,128]{3,2,1,0:T(8,128)(2,1)} %get-tuple-element.485, s32[1024]{0:T(1024)S(1)} %pad_clamp_fusion.3), kind=kCustom, calls=%fused_computation.1.clone.clone.1 | custom fusion | bytes 33554688 | tf_op jit(solution)/shard_map/while/body/eval_jaxpr/jit(_take)/gather | solution.py:142
  260.0 7.4 %gather_fusion.1 = bf16[64,128,8,128]{3,2,1,0:T(8,128)(2,1)} fusion(bf16[8,128,8,128]{3,2,1,0:T(8,128)(2,1)S(1)} %get-tuple-element.486, s32[1024]{0:T(1024)S(1)} %pad_clamp_fusion.3), kind=kCustom, calls=%fused_computation.clone.clone.1 | custom fusion | bytes 33554688 | tf_op jit(solution)/shard_map/while/body/eval_jaxpr/jit(_take)/gather | solution.py:139
  267.4 23.2 %broadcast_select_fusion.5 = (bf16[64,128,8,128]{3,2,1,0:T(8,128)(2,1)}, bf16[64,128,8,128]{3,2,1,0:T(8,128)(2,1)}) fusion(bf16[64,128,8,128]{3,2,1,0:T(8,128)(2,1)} %gather_fusion, pred[64]{0:T(512)(128)(4,1)S(1)} %compare_and_fusion.3, bf16[64,128,8,128]{3,2,1,0:T(8,128)(2,1)} %gather_fusion.1), kind=kLoop, calls=%fused_computation.61.clone.1 | loop fusion | flops 16777216 | bytes 67108928 | tf_op jit(solution)/shard_map/while/body/eval_jaxpr/jit(_take)/select_n | solution.py:142
  290.8 19.7 %bitcast_reduce_fusion.2 = (f32[4,8,128]{2,1,0:T(8,128)S(1)}, f32[4,8,2048,128]{3,2,1,0:T(8,128)}) fusion(pred[4,2048]{1,0:T(4,128)(4,1)S(1)} %bitcast.199, bf16[1,4,128,8,1,128]{5,3,2,1,0,4:T(8,128)(2,1)S(1)} %constant_dynamic-slice_fusion.9, bf16[4,2048,8,128]{3,2,1,0:T(8,128)(2,1)} %bitcast.193), kind=kOutput, calls=%fused_computation.47.clone.1 | convolution fusion | flops 2172645376 | bytes 51404800 | tf_op jit(solution)/shard_map/while/body/eval_jaxpr/bqhgd,bkhd->bhgqk/dot_general | solution.py:146
  310.5 15.1 %fusion.72 = f32[4,8,128]{2,1,0:T(8,128)S(1)} fusion(f32[4,8,2048,128]{3,2,1,0:T(8,128)} %get-tuple-element.490, f32[4,8,128]{2,1,0:T(8,128)S(1)} %get-tuple-element.488, pred[4,2048]{1,0:T(4,128)(4,1)S(1)} %bitcast.200), kind=kLoop, calls=%fused_computation.51.clone.1 | loop fusion | flops 41938944 | bytes 33595392 | tf_op jit(solution)/shard_map/while/body/eval_jaxpr/reduce_sum | solution.py:34
  325.7 22.7 %bitcast_dynamic-update-slice_fusion.11 = f32[2,4,8,1,128,128]{5,4,2,1,3,0:T(8,128)} fusion(f32[2,4,8,1,128,128]{5,4,2,1,3,0:T(8,128)} %get-tuple-element.502, s32[]{:T(128)} %get-tuple-element.500, bf16[4,2048,8,128]{3,2,1,0:T(8,128)(2,1)} %bitcast.192, f32[4,8,2048,128]{3,2,1,0:T(8,128)} %get-tuple-element.490, ...), kind=kOutput, calls=%fused_computation.65.clone.1 | convolution fusion | flops 2189426688 | bytes 52462080 | tf_op jit(solution)/shard_map/while/body/eval_jaxpr/bhgqk,bkhd->bhgqd/dot_general | solution.py:155
  349.1 4.7 %copy.61 = f32[8,8,1,128,128]{4,1,3,0,2:T(8,128)S(1)} copy(f32[8,8,1,128,128]{4,3,1,0,2:T(8,128)} %bitcast.24) | data formatting | bytes 8388608 | tf_op jit(solution)/shard_map/reshape | solution.py:170
  353.8 5.8 %fusion.47 = bf16[1024,8,1,128]{3,1,2,0:T(8,128)(2,1)} fusion(f32[8,1024]{0,1:T(8,128)S(1)} %copy.63, f32[8,1,1024,128]{3,0,1,2:T(8,128)S(1)} %bitcast.196, f32[8,1024]{0,1:T(8,128)S(1)} %copy.60, f32[8,1,1024,128]{3,0,1,2:T(8,128)S(1)} %bitcast.195, f32[8,1024]{0,1:T(8,128)S(1)} %copy.58), kind=kLoop, calls=%fused_computation.90 | loop fusion | flops 5242880 | bytes 10584064 | tf_op jit(solution)/shard_map/convert_element_type | solution.py:180
  (99 shorter events, 6.9 us)
Async XLA Ops:
  1.9 5.1 %collective-permute-start = (bf16[1,1024,8,128]{3,1,2,0:T(8,128)(2,1)S(1)}, bf16[1,1024,8,128]{3,1,2,0:T(8,128)(2,1)}, u32[]{:S(2)}, u32[]{:S(2)}) collective-permute-start(bf16[1,1024,8,128]{3,1,2,0:T(8,128)(2,1)S(1)} %copy.46), channel_id=1, source_target_pairs={{0,1},{1,0},{2,3},{3,2},{4,5},{5,4},{6,7},{7,6},{8,9},{9,8},{10,11... | collective-permute-start | bytes 6291464 | tf_op jit(solution)/shard_map/ppermute | solution.py:21
  9.8 1.3 copy-start.1
  12.5 39.5 %collective-permute-start.1 = (bf16[2,384,8,128]{3,1,2,0:T(8,128)(2,1)}, bf16[2,384,8,128]{3,1,2,0:T(8,128)(2,1)}, u32[]{:S(2)}, u32[]{:S(2)}) collective-permute-start(bf16[2,384,8,128]{3,1,2,0:T(8,128)(2,1)} %fusion.48), channel_id=1, source_target_pairs={{0,4},{4,8},{8,12},{1,5},{5,9},{9,13},{2,6},{6,10},{10,14},{3,7},{... | collective-permute-start | bytes 4718600 | tf_op jit(solution)/shard_map/ppermute | solution.py:27
  14.1 0.6 copy-start.3
  31.2 110.0 %all-to-all-start = ((bf16[2,8,128,8,128]{4,3,2,0,1:T(8,128)(2,1)}), bf16[2,8,128,8,128]{4,3,2,0,1:T(8,128)(2,1)}, u32[]{:S(2)}, u32[]{:S(2)}) async-start(bf16[2,8,128,8,128]{4,3,2,0,1:T(8,128)(2,1)} %select_bitcast_fusion), calls=%async_computation | async-start | bytes 8388608 | tf_op jit(solution)/shard_map/all_to_all | solution.py:80
  129.8 16.0 %copy-start.6 = (f32[2,8,1,512,1]{3,1,4,2,0:T(8,128)}, f32[2,8,1,512,1]{3,1,4,2,0:T(8,128)S(1)}, u32[]{:S(2)}) copy-start(f32[2,8,1,512,1]{3,1,4,2,0:T(8,128)S(1)} %get-tuple-element.248) | copy-start | bytes 98308
  137.0 8.8 %copy-start.4 = (f32[2,4,8,1,128,1]{4,2,1,5,3,0:T(8,128)S(1)}, f32[2,4,8,1,128,1]{4,2,1,5,3,0:T(8,128)}, u32[]{:S(2)}) copy-start(f32[2,4,8,1,128,1]{4,2,1,5,3,0:T(8,128)} %copy-done.3) | copy-start | bytes 98308
  145.8 202.6 %copy-start.5 = (f32[1,8,2,512]{3,1,2,0:T(8,128)S(1)}, f32[1,8,2,512]{3,1,2,0:T(8,128)}, u32[]{:S(2)}) copy-start(f32[1,8,2,512]{3,1,2,0:T(8,128)} %copy.69) | copy-start | bytes 98308
  145.8 202.6 %copy-start.7 = (f32[2,8,1,512,1]{3,1,4,2,0:T(8,128)S(1)}, f32[2,8,1,512,1]{3,1,4,2,0:T(8,128)}, u32[]{:S(2)}) copy-start(f32[2,8,1,512,1]{3,1,4,2,0:T(8,128)} %copy-done.6) | copy-start | bytes 98308
  166.0 23.4 %copy-start = (bf16[2,4,128,8,1,128]{5,3,2,1,0,4:T(8,128)(2,1)S(1)}, bf16[2,4,128,8,1,128]{5,3,2,1,0,4:T(8,128)(2,1)}, u32[]{:S(2)}) copy-start(bf16[2,4,128,8,1,128]{5,3,2,1,0,4:T(8,128)(2,1)} %get-tuple-element.516) | copy-start | bytes 6291460 | tf_op jit(solution)/shard_map/while
  267.4 23.4 %copy-start = (bf16[2,4,128,8,1,128]{5,3,2,1,0,4:T(8,128)(2,1)S(1)}, bf16[2,4,128,8,1,128]{5,3,2,1,0,4:T(8,128)(2,1)}, u32[]{:S(2)}) copy-start(bf16[2,4,128,8,1,128]{5,3,2,1,0,4:T(8,128)(2,1)} %get-tuple-element.516) | copy-start | bytes 6291460 | tf_op jit(solution)/shard_map/while
  349.1 4.7 %copy-start.2 = (f32[8,1,2,512,128]{4,0,3,2,1:T(8,128)S(1)}, f32[8,1,2,512,128]{4,0,3,2,1:T(8,128)}, u32[]{:S(2)}) copy-start(f32[8,1,2,512,128]{4,0,3,2,1:T(8,128)} %copy.59) | copy-start | bytes 12582916
where the time goes:
time: 361 us; the launch traced here: 360 us
  matrix products  126 us (35%)
  other arithmetic  120 us (33%)
  local copies, waits for them, and re-layouts  79.6 us (22%)
  waiting for transfers between devices  16.6 us (5%)
  starting transfers between devices  9.72 us (3%)
  loops' own time  7.96 us (2%)
    reduce_sum x4, other arithmetic, group_weights(): return (summit, weights, jnp.sum(weights, axis=-1, keepdims=True))  47.6 us
    select_n x2, other arithmetic, far_group(): jnp.take(pool_pair[1], slot_tile.reshape(-1), axis=0)  46.4 us
    dot_general x2, matrix products, far_group(): jnp.einsum('bhgqk,bkhd->bhgqd', weights.astype(jnp.bfloat16), value_tile,...  45.4 us
    dot_general x2, matrix products, far_group(): jnp.einsum('bqhgd,bkhd->bhgqk', query_tile, keys_tile, preferred_element_...  39.4 us
    dot_general x2, matrix products, near_part(): jnp.einsum('hgqk,khd->hgqd', weights.astype(jnp.bfloat16), pair_tile[1],...  24 us
    gather x2, local copies, waits for them, and re-layouts, far_group(): jnp.take(pool_pair[1], slot_tile.reshape(-1), axis=0)  17.8 us
    dot_general x2, matrix products, near_part(): jnp.einsum('qhgd,khd->hgqk', query_tile, pair_tile[0], preferred_element_...  16.8 us
    gather x2, local copies, waits for them, and re-layouts, far_group(): jnp.take(pool_pair[0], slot_tile.reshape(-1), axis=0)  14.6 us
  transfers between devices with their start and end apart: 3, of which 2 were waited for; matrix products, arithmetic and copies ran while one was open for 28% of the time, Pallas kernels for 0%

commit v1 on v0

--- a/solution.py
+++ b/solution.py
@@ -77,8 +77,15 @@
     slot_width = CAP
     rim_pair = from_behind(local_pair[:, rim_start:], "ctx", 1)
     blocked = local_pair.reshape(local_pair.shape[0], own_blocks, block_len, head_count, head_width)
-    pool_pair = lax.all_to_all(
-        jnp.take(blocked, send_index, axis=1), "ctx", split_axis=1, concat_axis=1, tiled=True
+    arr = jnp.take(blocked, send_index, axis=1)
+    pool_pair = jnp.concatenate(
+        lax.all_to_all(
+            jnp.stack(jnp.split(arr, lax.axis_size("ctx"), 1), 0),
+            "ctx",
+            split_axis=0,
+            concat_axis=0,
+        ),
+        1,
     )
     my_list = lax.dynamic_slice_in_dim(far_list, my_span * own_blocks, own_blocks, 0)
     my_count = lax.dynamic_slice_in_dim(far_count, my_span * own_blocks, own_blocks, 0)

time: 361 us -> 372 us (1.030); the launches traced: 360 us -> 365 us
  loops' own time: 7.96 us -> 17.9 us
    another operation x1, loops' own time: 7.85 us -> 17.8 us  [local(): near_top, near_out, near_sum = lax.map(near_part, starts)]
    all_to_all x1, waiting for transfers between devices: 4.25 us -> 0.01 us  [local(): lax.all_to_all(jnp.stack(jnp.split(arr, lax.axis_size('ctx'), 1), 0), 'ct...]
  transfers between devices with their start and end apart: 3 -> 3, of which waited for: 2 -> 1; matrix products, arithmetic and copies ran while one was open for 28% -> 27% of each run, Pallas kernels for 0% -> 0%
where the time goes in v1:
time: 372 us; the launch traced here: 365 us
  matrix products  126 us (34%)
  other arithmetic  119 us (32%)
  local copies, waits for them, and re-layouts  78.6 us (21%)
  loops' own time  17.9 us (5%)
  waiting for transfers between devices  13.8 us (4%)
  starting transfers between devices  10.2 us (3%)
    reduce_sum x4, other arithmetic, group_weights(): return (summit, weights, jnp.sum(weights, axis=-1, keepdims=True))  47.6 us
    select_n x2, other arithmetic, far_group(): jnp.take(pool_pair[1], slot_tile.reshape(-1), axis=0)  46.4 us
    dot_general x2, matrix products, far_group(): jnp.einsum('bhgqk,bkhd->bhgqd', weights.astype(jnp.bfloat16), value_tile,...  45.4 us
    dot_general x2, matrix products, far_group(): jnp.einsum('bqhgd,bkhd->bhgqk', query_tile, keys_tile, preferred_element_...  39.4 us
    dot_general x2, matrix products, near_part(): jnp.einsum('hgqk,khd->hgqd', weights.astype(jnp.bfloat16), pair_tile[1],...  24.1 us
    gather x2, local copies, waits for them, and re-layouts, far_group(): jnp.take(pool_pair[1], slot_tile.reshape(-1), axis=0)  17.8 us
    another operation x1, loops' own time, local(): near_top, near_out, near_sum = lax.map(near_part, starts)  17.8 us
    dot_general x2, matrix products, near_part(): jnp.einsum('qhgd,khd->hgqk', query_tile, pair_tile[0], preferred_element_...  16.8 us
  transfers between devices with their start and end apart: 3, of which 1 were waited for; matrix products, arithmetic and copies ran while one was open for 27% of the time, Pallas kernels for 0%

profile of v1, /device:TPU:24, one launch (start us, length us, event | category | flops | bytes accessed | tf_op | source)
XLA Modules:
  0.0 365.3 jit_solution(6261218820661865833)
XLA Ops:
  0.0 1.9 copy.49
  2.0 0.7 lt.111
  2.9 0.8 copy.53
  4.6 0.7 dynamic_slice.49
  5.6 0.8 constant_dynamic-slice_fusion.4
  8.0 2.9 broadcast_select_fusion.3
  10.8 1.4 fusion.48
  12.2 1.3 collective-permute-start.1
  13.9 4.6 %copy.55 = bf16[2,1024,8,128]{3,2,1,0:T(8,128)(2,1)} copy(bf16[2,1024,8,128]{3,1,2,0:T(8,128)(2,1)S(1)} %pad_maximum_fusion) | data formatting | bytes 8388608 | tf_op jit(solution)/shard_map/concatenate | solution.py:53
  18.6 5.2 %gather_fusion.2 = bf16[8,2,128,8,128]{4,3,2,1,0:T(8,128)(2,1)} fusion(bf16[2,8,128,8,128]{4,3,2,1,0:T(8,128)(2,1)} %bitcast.208, s32[1024]{0:T(1024)S(1)} %pad_clamp_fusion.1), kind=kCustom, calls=%fused_computation.2 | custom fusion | bytes 8388640 | tf_op jit(solution)/shard_map/jit(_take)/gather | solution.py:80
  23.8 2.7 select_bitcast_fusion
  26.8 2.3 pad_maximum_fusion.1
  29.1 8.8 %all-to-all-start = ((bf16[4,2,2,128,8,128]{5,4,3,1,2,0:T(8,128)(2,1)}), bf16[4,2,2,128,8,128]{5,4,3,1,2,0:T(8,128)(2,1)}, u32[]{:S(2)}, u32[]{:S(2)}) async-start(bf16[4,2,2,128,8,128]{5,4,3,1,2,0:T(8,128)(2,1)} %pad_maximum_fusion.1), calls=%async_computation | async-start | bytes 8388608 | tf_op jit(solution)/shard_map/all_to_all | solution.py:82
  37.9 13.8 %collective-permute-done.1 = bf16[2,384,8,128]{3,1,2,0:T(8,128)(2,1)} collective-permute-done((bf16[2,384,8,128]{3,1,2,0:T(8,128)(2,1)}, bf16[2,384,8,128]{3,1,2,0:T(8,128)(2,1)}, u32[]{:S(2)}, u32[]{:S(2)}) %collective-permute-start.1) | collective-permute-done | bytes 1572896 | tf_op jit(solution)/shard_map/ppermute | solution.py:27
  51.7 4.9 %maximum_maximum_fusion = bf16[2,1408,8,128]{3,1,2,0:T(8,128)(2,1)} fusion(bf16[1,1024,8,128]{3,1,2,0:T(8,128)(2,1)} %copy-done.1, bf16[1,1024,8,128]{3,1,2,0:T(8,128)(2,1)S(1)} %get-tuple-element.371, bf16[2,384,8,128]{3,1,2,0:T(8,128)(2,1)} %collective-permute-done.1), kind=kLoop, calls=%fused_computation.84 | loop fusion | flops 17301504 | bytes 11534336 | tf_op jit(solution)/shard_map/concatenate | solution.py:93
  56.6 82.9 %while.34 = (s32[]{:T(128)}, f32[2,8,1,512,1]{3,1,4,2,0:T(8,128)S(1)}, f32[2,8,1,512,128]{4,3,1,2,0:T(8,128)}, f32[2,8,1,512,1]{3,4,2,1,0:T(1,128)S(1)}, s32[2]{...) while((s32[]{:T(128)}, ...), condition=%wide.region_3.4_spmd, body=%wide.region_0.3_spmd.sunk | while | flops 1928610944 | bytes 54944268 | solution.py:124
  57.9 0.7 fusion.66
  58.6 0.9 and_and_fusion.2
  61.4 1.3 constant_dynamic-slice_fusion.8
  64.0 8.4 %fusion.67 = (f32[8,512]{1,0:T(8,128)S(1)}, f32[8,896,512]{2,1,0:T(8,128)}) fusion(pred[512,896]{0,1:T(8,128)(4,1)S(1)} %and_and_fusion.2, bf16[512,8,1,128]{3,1,2,0:T(8,128)(2,1)S(1)} %constant_dynamic-slice_fusion.8, bf16[2,1408,8,128]{3,1,2,0:T(8,128)(2,1)} %get-tuple-element.556, s32[]{:T(128)S(6)} %select_n.250), kind=kOutput, calls=%fused_computation.6.clone.1 | convolution fusion | flops 950530048 | bytes 18038788 | tf_op jit(solution)/shard_map/while/body/eval_jaxpr/qhgd,khd->hgqk/dot_general | solution.py:102
  72.4 8.7 %fusion.68 = f32[8,512]{1,0:T(8,128)S(1)} fusion(f32[8,896,512]{2,1,0:T(8,128)} %get-tuple-element.480, f32[8,512]{1,0:T(8,128)S(1)} %get-tuple-element.479, pred[512,896]{0,1:T(8,128)(4,1)S(1)} %and_and_fusion.2), kind=kLoop, calls=%fused_computation.7.clone.1 | loop fusion | flops 18345984 | bytes 15171584 | tf_op jit(solution)/shard_map/while/body/eval_jaxpr/reduce_sum | solution.py:34
  81.1 12.1 %bitcast_dynamic-update-slice_fusion.9 = f32[2,8,1,512,128]{4,3,1,2,0:T(8,128)} fusion(f32[2,8,1,512,128]{4,3,1,2,0:T(8,128)} %get-tuple-element.538, s32[]{:T(128)} %get-tuple-element.536, bf16[2,1408,8,128]{3,1,2,0:T(8,128)(2,1)} %get-tuple-element.556, s32[]{:T(128)S(6)} %add.369, s32[]{:T(128)S(6)} %select_n.250, ...), kind=kOutput, calls=%fused_computation.12.clone.1 | convolution fusion | flops 957874176 | bytes 19087880 | tf_op jit(solution)/shard_map/while/body/eval_jaxpr/hgqk,khd->hgqd/dot_general | solution.py:115
  94.4 0.7 fusion.66
  95.1 0.9 and_and_fusion.2
  97.9 1.3 constant_dynamic-slice_fusion.8
  100.5 8.4 %fusion.67 = (f32[8,512]{1,0:T(8,128)S(1)}, f32[8,896,512]{2,1,0:T(8,128)}) fusion(pred[512,896]{0,1:T(8,128)(4,1)S(1)} %and_and_fusion.2, bf16[512,8,1,128]{3,1,2,0:T(8,128)(2,1)S(1)} %constant_dynamic-slice_fusion.8, bf16[2,1408,8,128]{3,1,2,0:T(8,128)(2,1)} %get-tuple-element.556, s32[]{:T(128)S(6)} %select_n.250), kind=kOutput, calls=%fused_computation.6.clone.1 | convolution fusion | flops 950530048 | bytes 18038788 | tf_op jit(solution)/shard_map/while/body/eval_jaxpr/qhgd,khd->hgqk/dot_general | solution.py:102
  108.9 8.7 %fusion.68 = f32[8,512]{1,0:T(8,128)S(1)} fusion(f32[8,896,512]{2,1,0:T(8,128)} %get-tuple-element.480, f32[8,512]{1,0:T(8,128)S(1)} %get-tuple-element.479, pred[512,896]{0,1:T(8,128)(4,1)S(1)} %and_and_fusion.2), kind=kLoop, calls=%fused_computation.7.clone.1 | loop fusion | flops 18345984 | bytes 15171584 | tf_op jit(solution)/shard_map/while/body/eval_jaxpr/reduce_sum | solution.py:34
  117.6 12.0 %bitcast_dynamic-update-slice_fusion.9 = f32[2,8,1,512,128]{4,3,1,2,0:T(8,128)} fusion(f32[2,8,1,512,128]{4,3,1,2,0:T(8,128)} %get-tuple-element.538, s32[]{:T(128)} %get-tuple-element.536, bf16[2,1408,8,128]{3,1,2,0:T(8,128)(2,1)} %get-tuple-element.556, s32[]{:T(128)S(6)} %add.369, s32[]{:T(128)S(6)} %select_n.250, ...), kind=kOutput, calls=%fused_computation.12.clone.1 | convolution fusion | flops 957874176 | bytes 19087880 | tf_op jit(solution)/shard_map/while/body/eval_jaxpr/hgqk,khd->hgqd/dot_general | solution.py:115
  139.6 0.6 copy.72
  140.2 6.5 %copy.62 = f32[8,1,2,512,128]{4,0,3,2,1:T(8,128)} copy(f32[8,1,2,512,128]{4,3,0,1,2:T(8,128)} %bitcast.209) | data formatting | bytes 8388608 | tf_op jit(solution)/shard_map/transpose | solution.py:38
  146.7 4.6 %copy.59 = bf16[2,8,128,8,128]{4,3,2,1,0:T(8,128)(2,1)} copy(bf16[2,8,128,8,128]{4,3,2,0,1:T(8,128)(2,1)} %bitcast.21) | data formatting | bytes 8388608
  151.3 202.6 %while.35 = (s32[]{:T(128)}, f32[2,4,8,1,128,1]{4,2,1,5,3,0:T(8,128)S(1)}, f32[2,4,8,1,128,128]{5,4,2,1,3,0:T(8,128)}, f32[2,4,8,1,128,1]{4,5,3,2,1,0:T(1,128)S(...) while((s32[]{:T(128)}, ...), condition=%wide.region_13.15_spmd.clone, body=%wide.region_10.14_spmd.clone.sunk | while | flops 4420789760 | bytes 290651552 | solution.py:175
  151.4 3.9 %slice_bitcast_fusion.7 = (bf16[8,128,8,128]{3,2,1,0:T(8,128)(2,1)}, bf16[8,128,8,128]{3,2,1,0:T(8,128)(2,1)S(1)}) fusion(bf16[2,8,128,8,128]{4,3,2,1,0:T(8,128)(2,1)} %get-tuple-element.518), kind=kLoop, calls=%fused_computation.66.clone.1 | loop fusion | bytes 8388608 | tf_op jit(solution)/shard_map/while/body/eval_jaxpr/squeeze | solution.py:149
  155.3 8.9 %gather_fusion = bf16[64,128,8,128]{3,2,1,0:T(8,128)(2,1)} fusion(bf16[8,128,8,128]{3,2,1,0:T(8,128)(2,1)} %get-tuple-element.489, s32[1024]{0:T(1024)S(1)} %pad_clamp_fusion.3), kind=kCustom, calls=%fused_computation.1.clone.clone.1 | custom fusion | bytes 33554688 | tf_op jit(solution)/shard_map/while/body/eval_jaxpr/jit(_take)/gather | solution.py:149
  164.2 7.3 %gather_fusion.1 = bf16[64,128,8,128]{3,2,1,0:T(8,128)(2,1)} fusion(bf16[8,128,8,128]{3,2,1,0:T(8,128)(2,1)S(1)} %get-tuple-element.490, s32[1024]{0:T(1024)S(1)} %pad_clamp_fusion.3), kind=kCustom, calls=%fused_computation.clone.clone.1 | custom fusion | bytes 33554688 | tf_op jit(solution)/shard_map/while/body/eval_jaxpr/jit(_take)/gather | solution.py:146
  171.5 23.2 %broadcast_select_fusion.5 = (bf16[64,128,8,128]{3,2,1,0:T(8,128)(2,1)}, bf16[64,128,8,128]{3,2,1,0:T(8,128)(2,1)}) fusion(bf16[64,128,8,128]{3,2,1,0:T(8,128)(2,1)} %gather_fusion, pred[64]{0:T(512)(128)(4,1)S(1)} %compare_and_fusion.3, bf16[64,128,8,128]{3,2,1,0:T(8,128)(2,1)} %gather_fusion.1), kind=kLoop, calls=%fused_computation.61.clone.1 | loop fusion | flops 16777216 | bytes 67108928 | tf_op jit(solution)/shard_map/while/body/eval_jaxpr/jit(_take)/select_n | solution.py:149
  195.0 19.7 %bitcast_reduce_fusion.2 = (f32[4,8,128]{2,1,0:T(8,128)S(1)}, f32[4,8,2048,128]{3,2,1,0:T(8,128)}) fusion(pred[4,2048]{1,0:T(4,128)(4,1)S(1)} %bitcast.210, bf16[1,4,128,8,1,128]{5,3,2,1,0,4:T(8,128)(2,1)S(1)} %constant_dynamic-slice_fusion.9, bf16[4,2048,8,128]{3,2,1,0:T(8,128)(2,1)} %bitcast.204), kind=kOutput, calls=%fused_computation.47.clone.1 | convolution fusion | flops 2172645376 | bytes 51404800 | tf_op jit(solution)/shard_map/while/body/eval_jaxpr/bqhgd,bkhd->bhgqk/dot_general | solution.py:153
  214.7 15.1 %fusion.72 = f32[4,8,128]{2,1,0:T(8,128)S(1)} fusion(f32[4,8,2048,128]{3,2,1,0:T(8,128)} %get-tuple-element.494, f32[4,8,128]{2,1,0:T(8,128)S(1)} %get-tuple-element.492, pred[4,2048]{1,0:T(4,128)(4,1)S(1)} %bitcast.211), kind=kLoop, calls=%fused_computation.51.clone.1 | loop fusion | flops 41938944 | bytes 33595392 | tf_op jit(solution)/shard_map/while/body/eval_jaxpr/reduce_sum | solution.py:34
  229.8 22.7 %bitcast_dynamic-update-slice_fusion.11 = f32[2,4,8,1,128,128]{5,4,2,1,3,0:T(8,128)} fusion(f32[2,4,8,1,128,128]{5,4,2,1,3,0:T(8,128)} %get-tuple-element.506, s32[]{:T(128)} %get-tuple-element.504, bf16[4,2048,8,128]{3,2,1,0:T(8,128)(2,1)} %bitcast.203, f32[4,8,2048,128]{3,2,1,0:T(8,128)} %get-tuple-element.494, ...), kind=kOutput, calls=%fused_computation.65.clone.1 | convolution fusion | flops 2189426688 | bytes 52462080 | tf_op jit(solution)/shard_map/while/body/eval_jaxpr/bhgqk,bkhd->bhgqd/dot_general | solution.py:162
  252.6 3.9 %slice_bitcast_fusion.7 = (bf16[8,128,8,128]{3,2,1,0:T(8,128)(2,1)}, bf16[8,128,8,128]{3,2,1,0:T(8,128)(2,1)S(1)}) fusion(bf16[2,8,128,8,128]{4,3,2,1,0:T(8,128)(2,1)} %get-tuple-element.518), kind=kLoop, calls=%fused_computation.66.clone.1 | loop fusion | bytes 8388608 | tf_op jit(solution)/shard_map/while/body/eval_jaxpr/squeeze | solution.py:149
  256.5 8.9 %gather_fusion = bf16[64,128,8,128]{3,2,1,0:T(8,128)(2,1)} fusion(bf16[8,128,8,128]{3,2,1,0:T(8,128)(2,1)} %get-tuple-element.489, s32[1024]{0:T(1024)S(1)} %pad_clamp_fusion.3), kind=kCustom, calls=%fused_computation.1.clone.clone.1 | custom fusion | bytes 33554688 | tf_op jit(solution)/shard_map/while/body/eval_jaxpr/jit(_take)/gather | solution.py:149
  265.5 7.4 %gather_fusion.1 = bf16[64,128,8,128]{3,2,1,0:T(8,128)(2,1)} fusion(bf16[8,128,8,128]{3,2,1,0:T(8,128)(2,1)S(1)} %get-tuple-element.490, s32[1024]{0:T(1024)S(1)} %pad_clamp_fusion.3), kind=kCustom, calls=%fused_computation.clone.clone.1 | custom fusion | bytes 33554688 | tf_op jit(solution)/shard_map/while/body/eval_jaxpr/jit(_take)/gather | solution.py:146
  272.9 23.2 %broadcast_select_fusion.5 = (bf16[64,128,8,128]{3,2,1,0:T(8,128)(2,1)}, bf16[64,128,8,128]{3,2,1,0:T(8,128)(2,1)}) fusion(bf16[64,128,8,128]{3,2,1,0:T(8,128)(2,1)} %gather_fusion, pred[64]{0:T(512)(128)(4,1)S(1)} %compare_and_fusion.3, bf16[64,128,8,128]{3,2,1,0:T(8,128)(2,1)} %gather_fusion.1), kind=kLoop, calls=%fused_computation.61.clone.1 | loop fusion | flops 16777216 | bytes 67108928 | tf_op jit(solution)/shard_map/while/body/eval_jaxpr/jit(_take)/select_n | solution.py:149
  296.3 19.7 %bitcast_reduce_fusion.2 = (f32[4,8,128]{2,1,0:T(8,128)S(1)}, f32[4,8,2048,128]{3,2,1,0:T(8,128)}) fusion(pred[4,2048]{1,0:T(4,128)(4,1)S(1)} %bitcast.210, bf16[1,4,128,8,1,128]{5,3,2,1,0,4:T(8,128)(2,1)S(1)} %constant_dynamic-slice_fusion.9, bf16[4,2048,8,128]{3,2,1,0:T(8,128)(2,1)} %bitcast.204), kind=kOutput, calls=%fused_computation.47.clone.1 | convolution fusion | flops 2172645376 | bytes 51404800 | tf_op jit(solution)/shard_map/while/body/eval_jaxpr/bqhgd,bkhd->bhgqk/dot_general | solution.py:153
  316.0 15.1 %fusion.72 = f32[4,8,128]{2,1,0:T(8,128)S(1)} fusion(f32[4,8,2048,128]{3,2,1,0:T(8,128)} %get-tuple-element.494, f32[4,8,128]{2,1,0:T(8,128)S(1)} %get-tuple-element.492, pred[4,2048]{1,0:T(4,128)(4,1)S(1)} %bitcast.211), kind=kLoop, calls=%fused_computation.51.clone.1 | loop fusion | flops 41938944 | bytes 33595392 | tf_op jit(solution)/shard_map/while/body/eval_jaxpr/reduce_sum | solution.py:34
  331.2 22.7 %bitcast_dynamic-update-slice_fusion.11 = f32[2,4,8,1,128,128]{5,4,2,1,3,0:T(8,128)} fusion(f32[2,4,8,1,128,128]{5,4,2,1,3,0:T(8,128)} %get-tuple-element.506, s32[]{:T(128)} %get-tuple-element.504, bf16[4,2048,8,128]{3,2,1,0:T(8,128)(2,1)} %bitcast.203, f32[4,8,2048,128]{3,2,1,0:T(8,128)} %get-tuple-element.494, ...), kind=kOutput, calls=%fused_computation.65.clone.1 | convolution fusion | flops 2189426688 | bytes 52462080 | tf_op jit(solution)/shard_map/while/body/eval_jaxpr/bhgqk,bkhd->bhgqd/dot_general | solution.py:162
  354.6 4.7 %copy.64 = f32[8,8,1,128,128]{4,1,3,0,2:T(8,128)S(1)} copy(f32[8,8,1,128,128]{4,3,1,0,2:T(8,128)} %bitcast.30) | data formatting | bytes 8388608 | tf_op jit(solution)/shard_map/reshape | solution.py:177
  359.3 5.8 %fusion.47 = bf16[1024,8,1,128]{3,1,2,0:T(8,128)(2,1)} fusion(f32[8,1024]{0,1:T(8,128)S(1)} %copy.66, f32[8,1,1024,128]{3,0,1,2:T(8,128)S(1)} %bitcast.207, f32[8,1024]{0,1:T(8,128)S(1)} %copy.63, f32[8,1,1024,128]{3,0,1,2:T(8,128)S(1)} %bitcast.206, f32[8,1024]{0,1:T(8,128)S(1)} %copy.61), kind=kLoop, calls=%fused_computation.91 | loop fusion | flops 5242880 | bytes 10584064 | tf_op jit(solution)/shard_map/convert_element_type | solution.py:187
  (101 shorter events, 6.4 us)
Async XLA Ops:
  1.9 6.1 %collective-permute-start = (bf16[1,1024,8,128]{3,1,2,0:T(8,128)(2,1)S(1)}, bf16[1,1024,8,128]{3,1,2,0:T(8,128)(2,1)}, u32[]{:S(2)}, u32[]{:S(2)}) collective-permute-start(bf16[1,1024,8,128]{3,1,2,0:T(8,128)(2,1)S(1)} %copy.49), channel_id=1, source_target_pairs={{0,1},{1,0},{2,3},{3,2},{4,5},{5,4},{6,7},{7,6},{8,9},{9,8},{10,11... | collective-permute-start | bytes 6291464 | tf_op jit(solution)/shard_map/ppermute | solution.py:21
  7.3 0.6 copy-start.3
  10.8 3.1 copy-start.1
  12.2 39.5 %collective-permute-start.1 = (bf16[2,384,8,128]{3,1,2,0:T(8,128)(2,1)}, bf16[2,384,8,128]{3,1,2,0:T(8,128)(2,1)}, u32[]{:S(2)}, u32[]{:S(2)}) collective-permute-start(bf16[2,384,8,128]{3,1,2,0:T(8,128)(2,1)} %fusion.48), channel_id=1, source_target_pairs={{0,4},{4,8},{8,12},{1,5},{5,9},{9,13},{2,6},{6,10},{10,14},{3,7},{... | collective-permute-start | bytes 4718600 | tf_op jit(solution)/shard_map/ppermute | solution.py:27
  29.1 117.6 %all-to-all-start = ((bf16[4,2,2,128,8,128]{5,4,3,1,2,0:T(8,128)(2,1)}), bf16[4,2,2,128,8,128]{5,4,3,1,2,0:T(8,128)(2,1)}, u32[]{:S(2)}, u32[]{:S(2)}) async-start(bf16[4,2,2,128,8,128]{5,4,3,1,2,0:T(8,128)(2,1)} %pad_maximum_fusion.1), calls=%async_computation | async-start | bytes 8388608 | tf_op jit(solution)/shard_map/all_to_all | solution.py:82
  139.5 11.8 %copy-start.6 = (f32[2,8,1,512,1]{3,1,4,2,0:T(8,128)}, f32[2,8,1,512,1]{3,1,4,2,0:T(8,128)S(1)}, u32[]{:S(2)}) copy-start(f32[2,8,1,512,1]{3,1,4,2,0:T(8,128)S(1)} %get-tuple-element.248) | copy-start | bytes 98308
  146.7 4.6 %copy-start.4 = (f32[2,4,8,1,128,1]{4,2,1,5,3,0:T(8,128)S(1)}, f32[2,4,8,1,128,1]{4,2,1,5,3,0:T(8,128)}, u32[]{:S(2)}) copy-start(f32[2,4,8,1,128,1]{4,2,1,5,3,0:T(8,128)} %copy-done.3) | copy-start | bytes 98308
  151.3 202.6 %copy-start.5 = (f32[1,8,2,512]{3,1,2,0:T(8,128)S(1)}, f32[1,8,2,512]{3,1,2,0:T(8,128)}, u32[]{:S(2)}) copy-start(f32[1,8,2,512]{3,1,2,0:T(8,128)} %copy.72) | copy-start | bytes 98308
  151.3 202.6 %copy-start.7 = (f32[2,8,1,512,1]{3,1,4,2,0:T(8,128)S(1)}, f32[2,8,1,512,1]{3,1,4,2,0:T(8,128)}, u32[]{:S(2)}) copy-start(f32[2,8,1,512,1]{3,1,4,2,0:T(8,128)} %copy-done.6) | copy-start | bytes 98308
  171.5 23.4 %copy-start = (bf16[2,4,128,8,1,128]{5,3,2,1,0,4:T(8,128)(2,1)S(1)}, bf16[2,4,128,8,1,128]{5,3,2,1,0,4:T(8,128)(2,1)}, u32[]{:S(2)}) copy-start(bf16[2,4,128,8,1,128]{5,3,2,1,0,4:T(8,128)(2,1)} %get-tuple-element.520) | copy-start | bytes 6291460 | tf_op jit(solution)/shard_map/while
  272.9 23.4 %copy-start = (bf16[2,4,128,8,1,128]{5,3,2,1,0,4:T(8,128)(2,1)S(1)}, bf16[2,4,128,8,1,128]{5,3,2,1,0,4:T(8,128)(2,1)}, u32[]{:S(2)}) copy-start(bf16[2,4,128,8,1,128]{5,3,2,1,0,4:T(8,128)(2,1)} %get-tuple-element.520) | copy-start | bytes 6291460 | tf_op jit(solution)/shard_map/while
  354.6 4.7 %copy-start.2 = (f32[8,1,2,512,128]{4,0,3,2,1:T(8,128)S(1)}, f32[8,1,2,512,128]{4,0,3,2,1:T(8,128)}, u32[]{:S(2)}) copy-start(f32[8,1,2,512,128]{4,0,3,2,1:T(8,128)} %copy.62) | copy-start | bytes 12582916
